TPU v7x, 512 devices: a whole 4x8x8 slice. The times are simulated.
512 devices in a mesh: tick: 64 (over y, z_hi, core), wire: 8 (over z_lo, x).
Axes of the slice: x: 4, y: 8, z: 8 (z_hi: 4, z_lo: 2; z = z_hi * 2 + z_lo), core: 2. Of those that a mesh axis runs over, the one named last changes fastest.
Arguments:
- signal: float32 [16, 512, 8192], P(None, 'wire', 'tick'), may hold values from -6 to 6
- kernel_front: float32 [16, 3, 9], replicated, may hold values from -1.25 to 1.25
- mixing_front: float32 [16, 16], replicated, may hold values from -1.5 to 1.5
- offset_front: float32 [16], replicated, may hold values from -2 to 2
- kernel_back: float32 [16, 3, 9], replicated, may hold values from -1.25 to 1.25
- mixing_back: float32 [16, 16], replicated, may hold values from -1.5 to 1.5
- offset_back: float32 [16], replicated, may hold values from -2 to 2
- upstream: float32 [16, 512, 8192], P(None, 'wire', 'tick'), may hold values from -13 to 13
Outputs:
- response: float32 [16, 512, 8192], P(None, 'wire', 'tick')
- signal_grad: float32 [16, 512, 8192], P(None, 'wire', 'tick')
- kernel_front_grad: float32 [16, 3, 9], replicated
- mixing_front_grad: float32 [16, 16], replicated
- offset_front_grad: float32 [16], replicated
- kernel_back_grad: float32 [16, 3, 9], replicated
- mixing_back_grad: float32 [16, 16], replicated
- offset_back_grad: float32 [16], replicated
All inputs are finite; a program needn't handle non-finite values.
Results may differ from a plain program's by a relative error of at most 0.0003.
Values sent between devices are 32-bit elements; how exact they have to be, the bound alone decides.
No kernel may reach another device: no remote copies, remote signals or barrier semaphores. Data moves between devices by JAX's collectives and lax.ppermute only.
A program may use at most 64 MiB of HBM per device.

v0:
```python
import math
import jax
import jax.numpy as jnp
from jax import lax
from jax.sharding import Mesh, PartitionSpec as P

TICK_DILATION = 8
TICK = ("y", "z_hi", "core")
WIRE = ("z_lo", "x")
REDUCTION_ORDER = ("core", "x", ("z_hi", "z_lo"), "y")


def with_halo(block, sides, width):
    for axis, dim in sides:
        count = lax.axis_size(axis)
        forward = [(i, i + 1) for i in range(count - 1)]
        backward = [(target, source) for source, target in forward]
        low = lax.ppermute(
            lax.slice_in_dim(block, block.shape[dim] - width, None, axis=dim), axis, forward
        )
        high = lax.ppermute(lax.slice_in_dim(block, 0, width, axis=dim), axis, backward)
        block = jnp.concatenate([low, block, high], axis=dim)
    return block


def spread(field, tick_deep, wire_deep):
    longer = with_halo(field, ((TICK, 2),), tick_deep)
    return with_halo(longer, ((WIRE, 1),), wire_deep)


def depthwise(padded_input, kernel_weight, row_count, column_count):
    total_sum = jnp.zeros((padded_input.shape[0], row_count, column_count), jnp.float32)
    for row_index in range(3):
        for column_index in range(9):
            total_sum = (
                total_sum
                + kernel_weight[:, row_index, column_index][:, None, None]
                * padded_input[
                    :,
                    row_index : row_index + row_count,
                    TICK_DILATION * column_index : TICK_DILATION * column_index + column_count,
                ]
            )
    return total_sum


def tap_grads(upward_gradient, padded_input):
    row_count = upward_gradient.shape[1]
    column_count = upward_gradient.shape[2]
    text_lines = []
    for row_index in range(3):
        text_lines.append(
            jnp.stack(
                [
                    jnp.sum(
                        upward_gradient
                        * padded_input[
                            :,
                            row_index : row_index + row_count,
                            TICK_DILATION * column_index : TICK_DILATION * column_index
                            + column_count,
                        ],
                        axis=(1, 2),
                    )
                    for column_index in range(9)
                ],
                axis=1,
            )
        )
    return jnp.stack(text_lines, axis=1)


def mixing(matrix, field, offset):
    return (
        jnp.einsum("oc,cwt->owt", matrix, field, precision=lax.Precision.HIGHEST)
        + offset[:, None, None]
    )


def slope(preact):
    sig = jax.nn.sigmoid(preact)
    return sig * (1.0 + preact * (1.0 - sig))


def per_device(
    signal,
    kernel_front,
    mixing_front,
    offset_front,
    kernel_back,
    mixing_back,
    offset_back,
    upstream,
):
    row_count = signal.shape[1]
    column_count = signal.shape[2]
    kernel_extent = 4 * TICK_DILATION
    padded_in = spread(signal, kernel_extent, 1)
    taps_front = depthwise(padded_in, kernel_front, row_count, column_count)
    pre_front = mixing(mixing_front, taps_front, offset_front)
    padded_act = spread(jax.nn.silu(pre_front), kernel_extent, 1)
    taps_back = depthwise(padded_act, kernel_back, row_count, column_count)
    pre_back = mixing(mixing_back, taps_back, offset_back)
    response = jax.nn.silu(pre_back)
    grad_back = upstream * slope(pre_back)
    gmix_back = jnp.einsum("owt,cwt->oc", grad_back, taps_back, precision=lax.Precision.HIGHEST)
    gbias_back = jnp.sum(grad_back, axis=(1, 2))
    under_back = jnp.einsum("oc,owt->cwt", mixing_back, grad_back, precision=lax.Precision.HIGHEST)
    gkern_back = tap_grads(under_back, padded_act)
    into_front = depthwise(
        spread(under_back, kernel_extent, 1), kernel_back[:, ::-1, ::-1], row_count, column_count
    )
    grad_front = into_front * slope(pre_front)
    gmix_front = jnp.einsum("owt,cwt->oc", grad_front, taps_front, precision=lax.Precision.HIGHEST)
    gbias_front = jnp.sum(grad_front, axis=(1, 2))
    under_front = jnp.einsum(
        "oc,owt->cwt", mixing_front, grad_front, precision=lax.Precision.HIGHEST
    )
    gkern_front = tap_grads(under_front, padded_in)
    signal_grad = depthwise(
        spread(under_front, kernel_extent, 1), kernel_front[:, ::-1, ::-1], row_count, column_count
    )
    totals = (gkern_front, gmix_front, gbias_front, gkern_back, gmix_back, gbias_back)
    packed = jnp.concatenate([item.reshape(-1) for item in totals])
    for group in REDUCTION_ORDER:
        packed = lax.psum(packed, group)
    sizes = [math.prod(item.shape) for item in totals]
    pieces = jnp.split(packed, [sum(sizes[: k + 1]) for k in range(len(sizes) - 1)])
    totals = [piece.reshape(item.shape) for piece, item in zip(pieces, totals)]
    factor = 1.0 / math.sqrt(row_count * lax.axis_size(WIRE) * column_count * lax.axis_size(TICK))
    return (
        response,
        signal_grad,
        totals[0] * factor,
        totals[1] * factor,
        totals[2] * factor,
        totals[3] * factor,
        totals[4] * factor,
        totals[5] * factor,
    )


def solution(mesh):
    fine = Mesh(mesh.devices.reshape(8, 4, 2, 2, 4), TICK + WIRE)
    block = P(None, WIRE, TICK)
    in_specs = (block, P(), P(), P(), P(), P(), P(), block)
    out_specs = (block, block, P(), P(), P(), P(), P(), P())
    return jax.shard_map(
        per_device, mesh=fine, in_specs=in_specs, out_specs=out_specs, check_vma=False
    )
```

profile of v0, /device:TPU:27, one launch (start us, length us, event | category | flops | bytes accessed | tf_op | source)
XLA Modules:
  0.0 215.1 jit_solution(8928391900136740163)
XLA Ops:
  0.6 1.4 constant_dynamic-update-slice_fusion.1
  2.2 6.4 %collective-permute-start = (f32[16,64,32]{2,0,1:T(8,128)S(1)}, f32[16,64,32]{2,0,1:T(8,128)S(1)}, u32[]{:S(2)}, u32[]{:S(2)}) collective-permute-start(f32[16,64,32]{2,0,1:T(8,128)S(1)} %get-tuple-element.133), channel_id=1, source_target_pairs={{0,8},{8,16},{16,24},{24,32},{32,40},{40,48},{48,56},{56,64},{64,7... | collective-permute-start | bytes 393224 | tf_op jit(solution)/shard_map/ppermute | solution.py:18
  8.6 1.9 collective-permute-start.1
  10.6 5.6 %collective-permute-done = f32[16,64,32]{2,0,1:T(8,128)S(1)} collective-permute-done((f32[16,64,32]{2,0,1:T(8,128)S(1)}, f32[16,64,32]{2,0,1:T(8,128)S(1)}, u32[]{:S(2)}, u32[]{:S(2)}) %collective-permute-start) | collective-permute-done | bytes 131104 | tf_op jit(solution)/shard_map/ppermute | solution.py:18
  16.2 12.0 %collective-permute-done.1 = f32[16,64,32]{2,0,1:T(8,128)S(1)} collective-permute-done((f32[16,64,32]{2,0,1:T(8,128)S(1)}, f32[16,64,32]{2,0,1:T(8,128)S(1)}, u32[]{:S(2)}, u32[]{:S(2)}) %collective-permute-start.1) | collective-permute-done | bytes 131104 | tf_op jit(solution)/shard_map/ppermute | solution.py:21
  28.3 3.1 %collective-permute-start.2 = (f32[16,1,192]{2,0,1:T(8,128)S(1)}, f32[16,1,192]{2,0,1:T(8,128)S(1)}, u32[]{:S(2)}, u32[]{:S(2)}) collective-permute-start(f32[16,1,192]{2,0,1:T(8,128)S(1)} %get-tuple-element.122), channel_id=1, source_target_pairs={{0,1},{1,2},{2,3},{3,4},{4,5},{5,6},{6,7},{8,9},{9,10},{10,11},{11... | collective-permute-start | bytes 36872 | tf_op jit(solution)/shard_map/ppermute | solution.py:18
  31.4 2.2 %collective-permute-start.3 = (f32[16,1,192]{2,0,1:T(8,128)S(1)}, f32[16,1,192]{2,0,1:T(8,128)S(1)}, u32[]{:S(2)}, u32[]{:S(2)}) collective-permute-start(f32[16,1,192]{2,0,1:T(8,128)S(1)} %get-tuple-element.123), channel_id=1, source_target_pairs={{1,0},{2,1},{3,2},{4,3},{5,4},{6,5},{7,6},{9,8},{10,9},{11,10},{12... | collective-permute-start | bytes 36872 | tf_op jit(solution)/shard_map/ppermute | solution.py:21
  33.6 2.2 %collective-permute-done.3 = f32[16,1,192]{2,0,1:T(8,128)S(1)} collective-permute-done((f32[16,1,192]{2,0,1:T(8,128)S(1)}, f32[16,1,192]{2,0,1:T(8,128)S(1)}, u32[]{:S(2)}, u32[]{:S(2)}) %collective-permute-start.3) | collective-permute-done | bytes 12320 | tf_op jit(solution)/shard_map/ppermute | solution.py:21
  35.9 0.9 maximum_maximum_fusion
  36.8 3.9 %multiply_add_fusion.1 = f32[16,64,128]{2,0,1:T(8,128)S(1)} fusion(f32[16,64,128]{2,0,1:T(8,128)S(1)} %get-tuple-element.132, f32[16,65,192]{2,0,1:T(8,128)S(1)} %get-tuple-element.121, f32[16,64,160]{2,0,1:T(8,128)S(1)} %constant_dynamic-update-slice_fusion, f32[16,65,192]{2,0,1:T(8,128)S(1)} %get-tuple-element.120, f32[16]{0:T(128)S(1)} %get-tuple-element.187, ...), kind=kLoop, calls=%fused_computation.251 | loop fusion | flops 7471104 | bytes 12715712 | tf_op jit(solution)/shard_map/add | solution.py:36
  40.8 1.4 fusion.93
  42.4 2.2 %collective-permute-start.4 = (f32[16,64,32]{2,0,1:T(8,128)S(1)}, f32[16,64,32]{2,0,1:T(8,128)S(1)}, u32[]{:S(2)}, u32[]{:S(2)}) collective-permute-start(f32[16,64,32]{2,0,1:T(8,128)S(1)} %get-tuple-element.129), channel_id=1, source_target_pairs={{0,8},{8,16},{16,24},{24,32},{32,40},{40,48},{48,56},{56,64},{64,7... | collective-permute-start | bytes 393224 | tf_op jit(solution)/shard_map/ppermute | solution.py:18
  44.6 2.2 %collective-permute-start.5 = (f32[16,64,32]{2,0,1:T(8,128)S(1)}, f32[16,64,32]{2,0,1:T(8,128)S(1)}, u32[]{:S(2)}, u32[]{:S(2)}) collective-permute-start(f32[16,64,32]{2,0,1:T(8,128)S(1)} %get-tuple-element.130), channel_id=1, source_target_pairs={{8,0},{16,8},{24,16},{32,24},{40,32},{48,40},{56,48},{64,56},{72,6... | collective-permute-start | bytes 393224 | tf_op jit(solution)/shard_map/ppermute | solution.py:21
  46.8 6.7 %collective-permute-done.4 = f32[16,64,32]{2,0,1:T(8,128)S(1)} collective-permute-done((f32[16,64,32]{2,0,1:T(8,128)S(1)}, f32[16,64,32]{2,0,1:T(8,128)S(1)}, u32[]{:S(2)}, u32[]{:S(2)}) %collective-permute-start.4) | collective-permute-done | bytes 131104 | tf_op jit(solution)/shard_map/ppermute | solution.py:18
  53.5 9.8 %collective-permute-done.5 = f32[16,64,32]{2,0,1:T(8,128)S(1)} collective-permute-done((f32[16,64,32]{2,0,1:T(8,128)S(1)}, f32[16,64,32]{2,0,1:T(8,128)S(1)}, u32[]{:S(2)}, u32[]{:S(2)}) %collective-permute-start.5) | collective-permute-done | bytes 131104 | tf_op jit(solution)/shard_map/ppermute | solution.py:21
  63.3 4.9 %collective-permute-start.6 = (f32[16,1,192]{2,0,1:T(8,128)S(1)}, f32[16,1,192]{2,0,1:T(8,128)S(1)}, u32[]{:S(2)}, u32[]{:S(2)}) collective-permute-start(f32[16,1,192]{2,0,1:T(8,128)S(1)} %get-tuple-element.118), channel_id=1, source_target_pairs={{0,1},{1,2},{2,3},{3,4},{4,5},{5,6},{6,7},{8,9},{9,10},{10,11},{11... | collective-permute-start | bytes 36872 | tf_op jit(solution)/shard_map/ppermute | solution.py:18
  68.3 1.9 collective-permute-start.7
  70.2 2.5 %collective-permute-done.7 = f32[16,1,192]{2,0,1:T(8,128)S(1)} collective-permute-done((f32[16,1,192]{2,0,1:T(8,128)S(1)}, f32[16,1,192]{2,0,1:T(8,128)S(1)}, u32[]{:S(2)}, u32[]{:S(2)}) %collective-permute-start.7) | collective-permute-done | bytes 12320 | tf_op jit(solution)/shard_map/ppermute | solution.py:21
  73.7 4.5 %multiply_add_fusion = f32[16,64,128]{2,0,1:T(8,128)S(1)} fusion(f32[16,64,128]{2,0,1:T(8,128)S(1)} %get-tuple-element.195, f32[16,65,192]{2,0,1:T(8,128)S(1)} %get-tuple-element.117, f32[16,65,192]{2,0,1:T(8,128)S(1)} %get-tuple-element.116, f32[16]{0:T(128)S(1)} %get-tuple-element.160, f32[16]{0:T(128)S(1)} %get-tuple-element.161, ...), kind=kLoop, calls=%fused_computation.248 | loop fusion | flops 7995392 | bytes 10749632 | tf_op jit(solution)/shard_map/add | solution.py:36
  78.2 1.8 fusion.98
  80.0 3.0 %multiply_reduce_fusion.18 = (f32[16]{0:T(128)S(1)}, f32[16]{0:T(128)S(1)}, f32[16]{0:T(128)S(1)}, f32[16]{0:T(128)S(1)}, f32[16]{0:T(128)S(1)}, /*index=5*/f32[...) fusion(f32[16,65,192]{2,0,1:T(8,128)S(1)} %get-tuple-element.11, ...), kind=kOutput, calls=%fused_computation.210 | convolution fusion | flops 29884128 | bytes 10487936 | tf_op jit(solution)/shard_map/oc,owt->cwt/dot_general | solution.py:108
  83.1 1.1 fusion.102
  84.2 2.1 collective-permute-start.8
  86.4 2.4 %collective-permute-start.9 = (f32[16,64,32]{2,0,1:T(8,128)}, f32[16,64,32]{2,0,1:T(8,128)}, u32[]{:S(2)}, u32[]{:S(2)}) collective-permute-start(f32[16,64,32]{2,0,1:T(8,128)} %get-tuple-element.127), channel_id=1, source_target_pairs={{8,0},{16,8},{24,16},{32,24},{40,32},{48,40},{56,48},{64,56},{72,6... | collective-permute-start | bytes 393224 | tf_op jit(solution)/shard_map/ppermute | solution.py:21
  88.8 5.1 %multiply_reduce_fusion.9 = (f32[16]{0:T(128)S(1)}, f32[16]{0:T(128)S(1)}, f32[16]{0:T(128)S(1)}, f32[16]{0:T(128)S(1)}, f32[16]{0:T(128)S(1)}, /*index=5*/f32[1...) fusion(f32[16,64,128]{2,0,1:T(8,128)} %copy-done.3, f32[16,64,32]{2,0,1:T(8,128)} %copy-done.8, ...), kind=kLoop, calls=%fused_computation.201 | loop fusion | flops 3932016 | bytes 1835584 | tf_op jit(solution)/shard_map/reduce_sum | solution.py:55
  94.0 2.0 convolution_bitcast_fusion.2
  96.0 2.5 %collective-permute-done.8 = f32[16,64,32]{2,0,1:T(8,128)} collective-permute-done((f32[16,64,32]{2,0,1:T(8,128)}, f32[16,64,32]{2,0,1:T(8,128)}, u32[]{:S(2)}, u32[]{:S(2)}) %collective-permute-start.8) | collective-permute-done | bytes 131104 | tf_op jit(solution)/shard_map/ppermute | solution.py:18
  98.5 8.5 %collective-permute-done.9 = f32[16,64,32]{2,0,1:T(8,128)} collective-permute-done((f32[16,64,32]{2,0,1:T(8,128)}, f32[16,64,32]{2,0,1:T(8,128)}, u32[]{:S(2)}, u32[]{:S(2)}) %collective-permute-start.9) | collective-permute-done | bytes 131104 | tf_op jit(solution)/shard_map/ppermute | solution.py:21
  107.8 2.3 %collective-permute-start.10 = (f32[16,1,192]{2,0,1:T(8,128)S(1)}, f32[16,1,192]{2,0,1:T(8,128)S(1)}, u32[]{:S(2)}, u32[]{:S(2)}) collective-permute-start(f32[16,1,192]{2,0,1:T(8,128)S(1)} %get-tuple-element.114), channel_id=1, source_target_pairs={{0,1},{1,2},{2,3},{3,4},{4,5},{5,6},{6,7},{8,9},{9,10},{10,11},{11... | collective-permute-start | bytes 36872 | tf_op jit(solution)/shard_map/ppermute | solution.py:18
  110.0 3.0 %collective-permute-start.11 = (f32[16,1,192]{2,0,1:T(8,128)S(1)}, f32[16,1,192]{2,0,1:T(8,128)S(1)}, u32[]{:S(2)}, u32[]{:S(2)}) collective-permute-start(f32[16,1,192]{2,0,1:T(8,128)S(1)} %get-tuple-element.115), channel_id=1, source_target_pairs={{1,0},{2,1},{3,2},{4,3},{5,4},{6,5},{7,6},{9,8},{10,9},{11,10},{12... | collective-permute-start | bytes 36872 | tf_op jit(solution)/shard_map/ppermute | solution.py:21
  113.4 2.0 copy.40
  115.4 2.5 %maximum_maximum_fusion.2 = (f32[16,65,192]{2,0,1:T(8,128)S(1)}, f32[16,65,192]{2,0,1:T(8,128)S(1)}) fusion(f32[16,64,32]{2,0,1:T(8,128)} %collective-permute-done.9, f32[16,64,128]{2,0,1:T(8,128)S(1)} %copy-done.4, f32[16,64,32]{2,0,1:T(8,128)} %collective-permute-done.8, f32[16,1,192]{2,0,1:T(8,128)S(1)} %collective-permute-done.10, ...), kind=kLoop, calls=%fused_computation.54 | loop fusion | flops 1198080 | bytes 2408448 | tf_op jit(solution)/shard_map/concatenate | solution.py:22
  117.9 6.5 %fusion.99 = (f32[16]{0:T(128)S(1)}, f32[16,64,128]{2,0,1:T(8,128)S(1)}) fusion(f32[16,64,128]{2,0,1:T(8,128)S(1)} %copy-done.13, f32[16,65,192]{2,0,1:T(8,128)S(1)} %get-tuple-element.113, f32[16]{0:T(128)S(1)} %get-tuple-element.135, f32[16]{0:T(128)S(1)} %get-tuple-element.154, f32[16]{0:T(128)S(1)} %get-tuple-element.159, f32[16]{0:T(128)S(1)} %get-tuple-element.158, ...), kind=kLoop, calls=%fused_computation.333 | loop fusion | flops 9175024 | bytes 11273984 | tf_op jit(solution)/shard_map/reduce_sum | solution.py:115
  125.2 3.0 %multiply_reduce_fusion.45 = (f32[16]{0:T(128)S(1)}, f32[16]{0:T(128)S(1)}, f32[16]{0:T(128)S(1)}, f32[16]{0:T(128)S(1)}, f32[16]{0:T(128)S(1)}, /*index=5*/f32[...) fusion(f32[16,65,192]{2,0,1:T(8,128)S(1)} %get-tuple-element.12, ...), kind=kOutput, calls=%fused_computation.237 | convolution fusion | flops 29884128 | bytes 10487936 | tf_op jit(solution)/shard_map/oc,owt->cwt/dot_general | solution.py:116
  128.3 1.1 fusion.101
  130.2 1.9 multiply_reduce_fusion.36
  132.5 2.5 %psum.28 = f32[1408]{0:T(1024)S(1)} all-reduce(f32[1408]{0:T(1024)S(1)} %concatenate.175), channel_id=1, replica_groups=mesh['y'=8,'z_hi'=4,'core'=2,'z_lo'=2,'x'=4] {'core'}, use_global_device_ids=true, to_apply=%region_56.57 | all-reduce | flops 1408 | bytes 11264 | tf_op jit(solution)/shard_map/psum | solution.py:126
  135.0 6.2 %psum.29 = f32[1408]{0:T(1024)S(1)} all-reduce(f32[1408]{0:T(1024)S(1)} %psum.28), channel_id=1, replica_groups=mesh['y'=8,'z_hi'=4,'core'=2,'z_lo'=2,'x'=4] {'x'}, use_global_device_ids=true, to_apply=%region_57.58 | all-reduce | flops 1408 | bytes 11264 | tf_op jit(solution)/shard_map/psum | solution.py:126
  141.2 15.5 %psum.30 = f32[1408]{0:T(1024)S(1)} all-reduce(f32[1408]{0:T(1024)S(1)} %psum.29), channel_id=1, replica_groups=mesh['y'=8,'z_hi'=4,'core'=2,'z_lo'=2,'x'=4] {'z_hi','z_lo'}, use_global_device_ids=true, to_apply=%region_58.59 | all-reduce | flops 1408 | bytes 11264 | tf_op jit(solution)/shard_map/psum | solution.py:126
  156.7 10.7 %psum.31 = f32[1408]{0:T(1024)S(1)} all-reduce(f32[1408]{0:T(1024)S(1)} %psum.30), channel_id=1, replica_groups=mesh['y'=8,'z_hi'=4,'core'=2,'z_lo'=2,'x'=4] {'y'}, use_global_device_ids=true, to_apply=%region_59.60 | all-reduce | flops 1408 | bytes 11264 | tf_op jit(solution)/shard_map/psum | solution.py:126
  167.5 11.2 %collective-permute-start.12 = (f32[16,64,32]{2,0,1:T(8,128)}, f32[16,64,32]{2,0,1:T(8,128)S(1)}, u32[]{:S(2)}, u32[]{:S(2)}) collective-permute-start(f32[16,64,32]{2,0,1:T(8,128)} %get-tuple-element.124), channel_id=1, source_target_pairs={{0,8},{8,16},{16,24},{24,32},{32,40},{40,48},{48,56},{56,64},{64,7... | collective-permute-start | bytes 393224 | tf_op jit(solution)/shard_map/ppermute | solution.py:18
  178.6 2.1 collective-permute-start.13
  180.8 9.9 %collective-permute-done.12 = f32[16,64,32]{2,0,1:T(8,128)S(1)} collective-permute-done((f32[16,64,32]{2,0,1:T(8,128)}, f32[16,64,32]{2,0,1:T(8,128)S(1)}, u32[]{:S(2)}, u32[]{:S(2)}) %collective-permute-start.12) | collective-permute-done | bytes 131104 | tf_op jit(solution)/shard_map/ppermute | solution.py:18
  190.7 8.8 %collective-permute-done.13 = f32[16,64,32]{2,0,1:T(8,128)S(1)} collective-permute-done((f32[16,64,32]{2,0,1:T(8,128)}, f32[16,64,32]{2,0,1:T(8,128)S(1)}, u32[]{:S(2)}, u32[]{:S(2)}) %collective-permute-start.13) | collective-permute-done | bytes 131104 | tf_op jit(solution)/shard_map/ppermute | solution.py:21
  199.6 1.9 collective-permute-start.14
  201.5 3.6 %collective-permute-start.15 = (f32[16,1,192]{2,0,1:T(8,128)S(1)}, f32[16,1,192]{2,0,1:T(8,128)S(1)}, u32[]{:S(2)}, u32[]{:S(2)}) collective-permute-start(f32[16,1,192]{2,0,1:T(8,128)S(1)} %get-tuple-element.111), channel_id=1, source_target_pairs={{1,0},{2,1},{3,2},{4,3},{5,4},{6,5},{7,6},{9,8},{10,9},{11,10},{12... | collective-permute-start | bytes 36872 | tf_op jit(solution)/shard_map/ppermute | solution.py:21
  209.6 4.5 %fusion.14 = f32[16,64,128]{2,0,1:T(8,128)S(1)} fusion(f32[16,64,128]{2,0,1:T(8,128)S(1)} %get-tuple-element.197, f32[16,64,32]{2,0,1:T(8,128)S(1)} %collective-permute-done.13, f32[16,64,32]{2,0,1:T(8,128)S(1)} %collective-permute-done.12, f32[16,65,192]{2,0,1:T(8,128)S(1)} %get-tuple-element.109, f32[16,65,192]{2,0,1:T(8,128)S(1)} %get-tuple-element.108, ...), kind=kLoop, calls=%fused_computation.70 | loop fusion | flops 7995392 | bytes 10749632 | tf_op jit(solution)/shard_map/add | solution.py:36
  214.1 1.0 copy.41
  (86 shorter events, 9.7 us)
Async XLA Ops:
  0.6 77.5 %copy-start = (f32[16,16]{1,0:T(8,128)S(1)}, f32[16,16]{1,0:T(8,128)}, u32[]{:S(2)}) copy-start(f32[16,16]{1,0:T(8,128)} %param.13) | copy-start | bytes 3076
  2.0 8.5 %copy-start.15 = (f32[16,3,9]{0,1,2:T(4,128)S(1)}, f32[16,3,9]{0,1,2:T(4,128)}, u32[]{:S(2)}) copy-start(f32[16,3,9]{0,1,2:T(4,128)} %param.9) | copy-start | bytes 5188
  2.2 14.0 %collective-permute-start = (f32[16,64,32]{2,0,1:T(8,128)S(1)}, f32[16,64,32]{2,0,1:T(8,128)S(1)}, u32[]{:S(2)}, u32[]{:S(2)}) collective-permute-start(f32[16,64,32]{2,0,1:T(8,128)S(1)} %get-tuple-element.133), channel_id=1, source_target_pairs={{0,8},{8,16},{16,24},{24,32},{32,40},{40,48},{48,56},{56,64},{64,7... | collective-permute-start | bytes 393224 | tf_op jit(solution)/shard_map/ppermute | solution.py:18
  8.6 19.6 %collective-permute-start.1 = (f32[16,64,32]{2,0,1:T(8,128)S(1)}, f32[16,64,32]{2,0,1:T(8,128)S(1)}, u32[]{:S(2)}, u32[]{:S(2)}) collective-permute-start(f32[16,64,32]{2,0,1:T(8,128)S(1)} %get-tuple-element.134), channel_id=1, source_target_pairs={{8,0},{16,8},{24,16},{32,24},{40,32},{48,40},{56,48},{64,56},{72,6... | collective-permute-start | bytes 393224 | tf_op jit(solution)/shard_map/ppermute | solution.py:21
  16.2 20.5 %copy-start.5 = (f32[16,64,32]{2,0,1:T(8,128)}, f32[16,64,32]{2,0,1:T(8,128)S(1)}, u32[]{:S(2)}) copy-start(f32[16,64,32]{2,0,1:T(8,128)S(1)} %collective-permute-done) | copy-start | bytes 393220
  28.3 5.4 %collective-permute-start.2 = (f32[16,1,192]{2,0,1:T(8,128)S(1)}, f32[16,1,192]{2,0,1:T(8,128)S(1)}, u32[]{:S(2)}, u32[]{:S(2)}) collective-permute-start(f32[16,1,192]{2,0,1:T(8,128)S(1)} %get-tuple-element.122), channel_id=1, source_target_pairs={{0,1},{1,2},{2,3},{3,4},{4,5},{5,6},{6,7},{8,9},{9,10},{10,11},{11... | collective-permute-start | bytes 36872 | tf_op jit(solution)/shard_map/ppermute | solution.py:18
  31.4 4.5 %collective-permute-start.3 = (f32[16,1,192]{2,0,1:T(8,128)S(1)}, f32[16,1,192]{2,0,1:T(8,128)S(1)}, u32[]{:S(2)}, u32[]{:S(2)}) collective-permute-start(f32[16,1,192]{2,0,1:T(8,128)S(1)} %get-tuple-element.123), channel_id=1, source_target_pairs={{1,0},{2,1},{3,2},{4,3},{5,4},{6,5},{7,6},{9,8},{10,9},{11,10},{12... | collective-permute-start | bytes 36872 | tf_op jit(solution)/shard_map/ppermute | solution.py:21
  33.6 3.1 %copy-start.1 = (f32[16,64,160]{2,0,1:T(8,128)}, f32[16,64,160]{2,0,1:T(8,128)S(1)}, u32[]{:S(2)}) copy-start(f32[16,64,160]{2,0,1:T(8,128)S(1)} %constant_dynamic-update-slice_fusion) | copy-start | bytes 1966084
  36.8 4.0 %copy-start.18 = (f32[16,16]{1,0:T(8,128)S(1)}, f32[16,16]{1,0:T(8,128)}, u32[]{:S(2)}) copy-start(f32[16,16]{1,0:T(8,128)} %param.10) | copy-start | bytes 3076
  36.8 4.0 %copy-start.19 = (f32[16]{0:T(128)S(1)}, f32[16]{0:T(128)}, u32[]{:S(2)}) copy-start(f32[16]{0:T(128)} %param.11) | copy-start | bytes 196
  40.8 1.4 copy-start.10
  42.2 4.5 %copy-start.16 = (f32[16,3,9]{0,1,2:T(4,128)S(1)}, f32[16,3,9]{0,1,2:T(4,128)}, u32[]{:S(2)}) copy-start(f32[16,3,9]{0,1,2:T(4,128)} %param.12) | copy-start | bytes 5188
  42.4 11.1 %collective-permute-start.4 = (f32[16,64,32]{2,0,1:T(8,128)S(1)}, f32[16,64,32]{2,0,1:T(8,128)S(1)}, u32[]{:S(2)}, u32[]{:S(2)}) collective-permute-start(f32[16,64,32]{2,0,1:T(8,128)S(1)} %get-tuple-element.129), channel_id=1, source_target_pairs={{0,8},{8,16},{16,24},{24,32},{32,40},{40,48},{48,56},{56,64},{64,7... | collective-permute-start | bytes 393224 | tf_op jit(solution)/shard_map/ppermute | solution.py:18
  44.6 18.7 %collective-permute-start.5 = (f32[16,64,32]{2,0,1:T(8,128)S(1)}, f32[16,64,32]{2,0,1:T(8,128)S(1)}, u32[]{:S(2)}, u32[]{:S(2)}) collective-permute-start(f32[16,64,32]{2,0,1:T(8,128)S(1)} %get-tuple-element.130), channel_id=1, source_target_pairs={{8,0},{16,8},{24,16},{32,24},{40,32},{48,40},{56,48},{64,56},{72,6... | collective-permute-start | bytes 393224 | tf_op jit(solution)/shard_map/ppermute | solution.py:21
  53.5 20.1 %copy-start.7 = (f32[16,64,32]{2,0,1:T(8,128)}, f32[16,64,32]{2,0,1:T(8,128)S(1)}, u32[]{:S(2)}) copy-start(f32[16,64,32]{2,0,1:T(8,128)S(1)} %collective-permute-done.4) | copy-start | bytes 393220
  63.3 10.4 %copy-start.8 = (f32[16,64,32]{2,0,1:T(8,128)}, f32[16,64,32]{2,0,1:T(8,128)S(1)}, u32[]{:S(2)}) copy-start(f32[16,64,32]{2,0,1:T(8,128)S(1)} %collective-permute-done.5) | copy-start | bytes 393220
  63.3 6.9 %collective-permute-start.6 = (f32[16,1,192]{2,0,1:T(8,128)S(1)}, f32[16,1,192]{2,0,1:T(8,128)S(1)}, u32[]{:S(2)}, u32[]{:S(2)}) collective-permute-start(f32[16,1,192]{2,0,1:T(8,128)S(1)} %get-tuple-element.118), channel_id=1, source_target_pairs={{0,1},{1,2},{2,3},{3,4},{4,5},{5,6},{6,7},{8,9},{9,10},{10,11},{11... | collective-permute-start | bytes 36872 | tf_op jit(solution)/shard_map/ppermute | solution.py:18
  68.3 4.5 %collective-permute-start.7 = (f32[16,1,192]{2,0,1:T(8,128)S(1)}, f32[16,1,192]{2,0,1:T(8,128)S(1)}, u32[]{:S(2)}, u32[]{:S(2)}) collective-permute-start(f32[16,1,192]{2,0,1:T(8,128)S(1)} %get-tuple-element.119), channel_id=1, source_target_pairs={{1,0},{2,1},{3,2},{4,3},{5,4},{6,5},{7,6},{9,8},{10,9},{11,10},{12... | collective-permute-start | bytes 36872 | tf_op jit(solution)/shard_map/ppermute | solution.py:21
  73.7 4.5 %copy-start.17 = (f32[16,64,128]{2,1,0:T(8,128)S(1)}, f32[16,64,128]{2,1,0:T(8,128)}, u32[]{:S(2)}) copy-start(f32[16,64,128]{2,1,0:T(8,128)} %param.15) | copy-start | bytes 1572868
  73.7 4.5 %copy-start.20 = (f32[16]{0:T(128)S(1)}, f32[16]{0:T(128)}, u32[]{:S(2)}) copy-start(f32[16]{0:T(128)} %param.14) | copy-start | bytes 196
  78.2 1.8 copy-start.12
  80.0 3.0 %copy-start.14 = (f32[16,64,128]{2,0,1:T(8,128)}, f32[16,64,128]{2,0,1:T(8,128)S(1)}, u32[]{:S(2)}) copy-start(f32[16,64,128]{2,0,1:T(8,128)S(1)} %get-tuple-element.105) | copy-start | bytes 1572868
  83.1 5.7 %copy-start.3 = (f32[16,64,128]{2,0,1:T(8,128)}, f32[16,64,128]{2,0,1:T(8,128)S(1)}, u32[]{:S(2)}) copy-start(f32[16,64,128]{2,0,1:T(8,128)S(1)} %get-tuple-element.198) | copy-start | bytes 1572868
  84.2 14.2 %collective-permute-start.8 = (f32[16,64,32]{2,0,1:T(8,128)}, f32[16,64,32]{2,0,1:T(8,128)}, u32[]{:S(2)}, u32[]{:S(2)}) collective-permute-start(f32[16,64,32]{2,0,1:T(8,128)} %get-tuple-element.126), channel_id=1, source_target_pairs={{0,8},{8,16},{16,24},{24,32},{32,40},{40,48},{48,56},{56,64},{64,7... | collective-permute-start | bytes 393224 | tf_op jit(solution)/shard_map/ppermute | solution.py:18
  86.4 20.5 %collective-permute-start.9 = (f32[16,64,32]{2,0,1:T(8,128)}, f32[16,64,32]{2,0,1:T(8,128)}, u32[]{:S(2)}, u32[]{:S(2)}) collective-permute-start(f32[16,64,32]{2,0,1:T(8,128)} %get-tuple-element.127), channel_id=1, source_target_pairs={{8,0},{16,8},{24,16},{32,24},{40,32},{48,40},{56,48},{64,56},{72,6... | collective-permute-start | bytes 393224 | tf_op jit(solution)/shard_map/ppermute | solution.py:21
  93.9 13.1 %copy-start.4 = (f32[16,64,128]{2,0,1:T(8,128)S(1)}, f32[16,64,128]{2,0,1:T(8,128)}, u32[]{:S(2)}) copy-start(f32[16,64,128]{2,0,1:T(8,128)} %copy-done.3) | copy-start | bytes 1572868
  107.8 7.6 %collective-permute-start.10 = (f32[16,1,192]{2,0,1:T(8,128)S(1)}, f32[16,1,192]{2,0,1:T(8,128)S(1)}, u32[]{:S(2)}, u32[]{:S(2)}) collective-permute-start(f32[16,1,192]{2,0,1:T(8,128)S(1)} %get-tuple-element.114), channel_id=1, source_target_pairs={{0,1},{1,2},{2,3},{3,4},{4,5},{5,6},{6,7},{8,9},{9,10},{10,11},{11... | collective-permute-start | bytes 36872 | tf_op jit(solution)/shard_map/ppermute | solution.py:18
  110.0 5.4 %collective-permute-start.11 = (f32[16,1,192]{2,0,1:T(8,128)S(1)}, f32[16,1,192]{2,0,1:T(8,128)S(1)}, u32[]{:S(2)}, u32[]{:S(2)}) collective-permute-start(f32[16,1,192]{2,0,1:T(8,128)S(1)} %get-tuple-element.115), channel_id=1, source_target_pairs={{1,0},{2,1},{3,2},{4,3},{5,4},{6,5},{7,6},{9,8},{10,9},{11,10},{12... | collective-permute-start | bytes 36872 | tf_op jit(solution)/shard_map/ppermute | solution.py:21
  115.4 2.5 %copy-start.13 = (f32[16,64,128]{2,0,1:T(8,128)S(1)}, f32[16,64,128]{2,0,1:T(8,128)}, u32[]{:S(2)}) copy-start(f32[16,64,128]{2,0,1:T(8,128)} %get-tuple-element.196) | copy-start | bytes 1572868
  117.9 6.5 %copy-start.11 = (f32[16,64,128]{2,0,1:T(8,128)S(1)}, f32[16,64,128]{2,0,1:T(8,128)}, u32[]{:S(2)}) copy-start(f32[16,64,128]{2,0,1:T(8,128)} %copy-done.10) | copy-start | bytes 1572868
  128.3 1.6 copy-start.2
  128.3 1.7 copy-start.6
  128.3 1.9 copy-start.9
  167.5 23.2 %collective-permute-start.12 = (f32[16,64,32]{2,0,1:T(8,128)}, f32[16,64,32]{2,0,1:T(8,128)S(1)}, u32[]{:S(2)}, u32[]{:S(2)}) collective-permute-start(f32[16,64,32]{2,0,1:T(8,128)} %get-tuple-element.124), channel_id=1, source_target_pairs={{0,8},{8,16},{16,24},{24,32},{32,40},{40,48},{48,56},{56,64},{64,7... | collective-permute-start | bytes 393224 | tf_op jit(solution)/shard_map/ppermute | solution.py:18
  178.6 20.9 %collective-permute-start.13 = (f32[16,64,32]{2,0,1:T(8,128)}, f32[16,64,32]{2,0,1:T(8,128)S(1)}, u32[]{:S(2)}, u32[]{:S(2)}) collective-permute-start(f32[16,64,32]{2,0,1:T(8,128)} %get-tuple-element.125), channel_id=1, source_target_pairs={{8,0},{16,8},{24,16},{32,24},{40,32},{48,40},{56,48},{64,56},{72,6... | collective-permute-start | bytes 393224 | tf_op jit(solution)/shard_map/ppermute | solution.py:21
  199.6 9.2 %collective-permute-start.14 = (f32[16,1,192]{2,0,1:T(8,128)S(1)}, f32[16,1,192]{2,0,1:T(8,128)S(1)}, u32[]{:S(2)}, u32[]{:S(2)}) collective-permute-start(f32[16,1,192]{2,0,1:T(8,128)S(1)} %get-tuple-element.110), channel_id=1, source_target_pairs={{0,1},{1,2},{2,3},{3,4},{4,5},{5,6},{6,7},{8,9},{9,10},{10,11},{11... | collective-permute-start | bytes 36872 | tf_op jit(solution)/shard_map/ppermute | solution.py:18
  201.5 7.2 %collective-permute-start.15 = (f32[16,1,192]{2,0,1:T(8,128)S(1)}, f32[16,1,192]{2,0,1:T(8,128)S(1)}, u32[]{:S(2)}, u32[]{:S(2)}) collective-permute-start(f32[16,1,192]{2,0,1:T(8,128)S(1)} %get-tuple-element.111), channel_id=1, source_target_pairs={{1,0},{2,1},{3,2},{4,3},{5,4},{6,5},{7,6},{9,8},{10,9},{11,10},{12... | collective-permute-start | bytes 36872 | tf_op jit(solution)/shard_map/ppermute | solution.py:21
where the time goes:
time: 216 us; the launch traced here: 215 us
  waiting for transfers between devices  68.6 us (32%)
  starting transfers between devices  53.2 us (25%)
  blocking collectives  34.9 us (16%)
  other arithmetic  33.2 us (15%)
  matrix products  12.1 us (6%)
  local copies, waits for them, and re-layouts  11.9 us (6%)
    ppermute x8, waiting for transfers between devices, with_halo(): lax.ppermute(lax.slice_in_dim(block, 0, width, axis=dim), axis, backward)  43.7 us
    psum x4, blocking collectives, per_device(): packed = lax.psum(packed, group)  34.9 us
    ppermute x8, starting transfers between devices, with_halo(): lax.ppermute(lax.slice_in_dim(block, block.shape[dim] - width, None, axis...  34.1 us
    ppermute x8, waiting for transfers between devices, with_halo(): lax.ppermute(lax.slice_in_dim(block, block.shape[dim] - width, None, axis...  24.8 us
    ppermute x8, starting transfers between devices, with_halo(): lax.ppermute(lax.slice_in_dim(block, 0, width, axis=dim), axis, backward)  19.2 us
    add x3, other arithmetic, depthwise(): total_sum + kernel_weight[:, row_index, column_index][:, None, None] * pa...  12.9 us
    reduce_sum x2, other arithmetic, tap_grads(): jnp.sum(upward_gradient * padded_input[:, row_index:row_index + row_count...  6.91 us
    unnamed x47, local copies, waits for them, and re-layouts  6.58 us
  transfers between devices with their start and end apart: 16, of which 10 were waited for; matrix products, arithmetic and copies ran while one was open for 6% of the time, Pallas kernels for 0%

commit v1 on v0

--- a/solution.py
+++ b/solution.py
@@ -123,7 +123,7 @@
     totals = (gkern_front, gmix_front, gbias_front, gkern_back, gmix_back, gbias_back)
     packed = jnp.concatenate([item.reshape(-1) for item in totals])
     for group in REDUCTION_ORDER:
-        packed = lax.psum(packed, group)
+        packed = jnp.sum(jax.lax.all_gather(packed, group), 0)
     sizes = [math.prod(item.shape) for item in totals]
     pieces = jnp.split(packed, [sum(sizes[: k + 1]) for k in range(len(sizes) - 1)])
     totals = [piece.reshape(item.shape) for piece, item in zip(pieces, totals)]

time: 216 us -> 237 us (1.097)
  the two profiles are of different devices: /device:TPU:27 before, /device:TPU:89 now
where the time goes in v1:
time: 237 us; the launch traced here: 236 us
  starting transfers between devices  73.9 us (31%)
  waiting for transfers between devices  51.6 us (22%)
  blocking collectives  50.6 us (21%)
  other arithmetic  34.6 us (15%)
  matrix products  12.1 us (5%)
  local copies, waits for them, and re-layouts  11.9 us (5%)
    all_gather x4, blocking collectives, per_device(): packed = jnp.sum(jax.lax.all_gather(packed, group), 0)  50.6 us
    ppermute x8, starting transfers between devices, with_halo(): lax.ppermute(lax.slice_in_dim(block, block.shape[dim] - width, None, axis...  37.2 us
    ppermute x8, starting transfers between devices, with_halo(): lax.ppermute(lax.slice_in_dim(block, 0, width, axis=dim), axis, backward)  36.7 us
    ppermute x8, waiting for transfers between devices, with_halo(): lax.ppermute(lax.slice_in_dim(block, block.shape[dim] - width, None, axis...  30.1 us
    ppermute x8, waiting for transfers between devices, with_halo(): lax.ppermute(lax.slice_in_dim(block, 0, width, axis=dim), axis, backward)  21.5 us
    add x3, other arithmetic, depthwise(): total_sum + kernel_weight[:, row_index, column_index][:, None, None] * pa...  12.9 us
    reduce_sum x2, other arithmetic, tap_grads(): jnp.sum(upward_gradient * padded_input[:, row_index:row_index + row_count...  6.91 us
    unnamed x55, local copies, waits for them, and re-layouts  6.61 us
  transfers between devices with their start and end apart: 16, of which 10 were waited for; matrix products, arithmetic and copies ran while one was open for 6% of the time, Pallas kernels for 0%

profile of v1, /device:TPU:89, one launch (start us, length us, event | category | flops | bytes accessed | tf_op | source)
XLA Modules:
  0.0 235.8 jit_solution(9214345651057739965)
XLA Ops:
  0.6 1.4 constant_dynamic-update-slice_fusion.1
  2.2 6.4 %collective-permute-start = (f32[16,64,32]{2,0,1:T(8,128)S(1)}, f32[16,64,32]{2,0,1:T(8,128)S(1)}, u32[]{:S(2)}, u32[]{:S(2)}) collective-permute-start(f32[16,64,32]{2,0,1:T(8,128)S(1)} %get-tuple-element.141), channel_id=1, source_target_pairs={{0,8},{8,16},{16,24},{24,32},{32,40},{40,48},{48,56},{56,64},{64,7... | collective-permute-start | bytes 393224 | tf_op jit(solution)/shard_map/ppermute | solution.py:18
  8.6 1.9 collective-permute-start.1
  10.6 8.9 %collective-permute-done = f32[16,64,32]{2,0,1:T(8,128)S(1)} collective-permute-done((f32[16,64,32]{2,0,1:T(8,128)S(1)}, f32[16,64,32]{2,0,1:T(8,128)S(1)}, u32[]{:S(2)}, u32[]{:S(2)}) %collective-permute-start) | collective-permute-done | bytes 131104 | tf_op jit(solution)/shard_map/ppermute | solution.py:18
  19.5 2.6 %collective-permute-done.1 = f32[16,64,32]{2,0,1:T(8,128)S(1)} collective-permute-done((f32[16,64,32]{2,0,1:T(8,128)S(1)}, f32[16,64,32]{2,0,1:T(8,128)S(1)}, u32[]{:S(2)}, u32[]{:S(2)}) %collective-permute-start.1) | collective-permute-done | bytes 131104 | tf_op jit(solution)/shard_map/ppermute | solution.py:21
  22.2 3.1 %collective-permute-start.2 = (f32[16,1,192]{2,0,1:T(8,128)S(1)}, f32[16,1,192]{2,0,1:T(8,128)S(1)}, u32[]{:S(2)}, u32[]{:S(2)}) collective-permute-start(f32[16,1,192]{2,0,1:T(8,128)S(1)} %get-tuple-element.130), channel_id=1, source_target_pairs={{0,1},{1,2},{2,3},{3,4},{4,5},{5,6},{6,7},{8,9},{9,10},{10,11},{11... | collective-permute-start | bytes 36872 | tf_op jit(solution)/shard_map/ppermute | solution.py:18
  25.3 8.4 %collective-permute-start.3 = (f32[16,1,192]{2,0,1:T(8,128)S(1)}, f32[16,1,192]{2,0,1:T(8,128)S(1)}, u32[]{:S(2)}, u32[]{:S(2)}) collective-permute-start(f32[16,1,192]{2,0,1:T(8,128)S(1)} %get-tuple-element.131), channel_id=1, source_target_pairs={{1,0},{2,1},{3,2},{4,3},{5,4},{6,5},{7,6},{9,8},{10,9},{11,10},{12... | collective-permute-start | bytes 36872 | tf_op jit(solution)/shard_map/ppermute | solution.py:21
  34.5 0.9 maximum_maximum_fusion
  35.4 3.9 %multiply_add_fusion.1 = f32[16,64,128]{2,0,1:T(8,128)S(1)} fusion(f32[16,64,128]{2,0,1:T(8,128)S(1)} %get-tuple-element.140, f32[16,65,192]{2,0,1:T(8,128)S(1)} %get-tuple-element.129, f32[16,64,160]{2,0,1:T(8,128)S(1)} %constant_dynamic-update-slice_fusion, f32[16,65,192]{2,0,1:T(8,128)S(1)} %get-tuple-element.128, f32[16]{0:T(128)S(1)} %get-tuple-element.195, ...), kind=kLoop, calls=%fused_computation.251 | loop fusion | flops 7471104 | bytes 12715712 | tf_op jit(solution)/shard_map/add | solution.py:36
  39.4 1.4 fusion.93
  41.0 1.9 collective-permute-start.4
  43.0 2.4 %collective-permute-start.5 = (f32[16,64,32]{2,0,1:T(8,128)S(1)}, f32[16,64,32]{2,0,1:T(8,128)S(1)}, u32[]{:S(2)}, u32[]{:S(2)}) collective-permute-start(f32[16,64,32]{2,0,1:T(8,128)S(1)} %get-tuple-element.138), channel_id=1, source_target_pairs={{8,0},{16,8},{24,16},{32,24},{40,32},{48,40},{56,48},{64,56},{72,6... | collective-permute-start | bytes 393224 | tf_op jit(solution)/shard_map/ppermute | solution.py:21
  45.4 9.3 %collective-permute-done.4 = f32[16,64,32]{2,0,1:T(8,128)S(1)} collective-permute-done((f32[16,64,32]{2,0,1:T(8,128)S(1)}, f32[16,64,32]{2,0,1:T(8,128)S(1)}, u32[]{:S(2)}, u32[]{:S(2)}) %collective-permute-start.4) | collective-permute-done | bytes 131104 | tf_op jit(solution)/shard_map/ppermute | solution.py:18
  54.7 7.7 %collective-permute-done.5 = f32[16,64,32]{2,0,1:T(8,128)S(1)} collective-permute-done((f32[16,64,32]{2,0,1:T(8,128)S(1)}, f32[16,64,32]{2,0,1:T(8,128)S(1)}, u32[]{:S(2)}, u32[]{:S(2)}) %collective-permute-start.5) | collective-permute-done | bytes 131104 | tf_op jit(solution)/shard_map/ppermute | solution.py:21
  62.5 1.9 collective-permute-start.6
  64.4 6.0 %collective-permute-start.7 = (f32[16,1,192]{2,0,1:T(8,128)S(1)}, f32[16,1,192]{2,0,1:T(8,128)S(1)}, u32[]{:S(2)}, u32[]{:S(2)}) collective-permute-start(f32[16,1,192]{2,0,1:T(8,128)S(1)} %get-tuple-element.127), channel_id=1, source_target_pairs={{1,0},{2,1},{3,2},{4,3},{5,4},{6,5},{7,6},{9,8},{10,9},{11,10},{12... | collective-permute-start | bytes 36872 | tf_op jit(solution)/shard_map/ppermute | solution.py:21
  71.3 0.9 maximum_maximum_fusion.1
  72.2 4.5 %multiply_add_fusion = f32[16,64,128]{2,0,1:T(8,128)S(1)} fusion(f32[16,64,128]{2,0,1:T(8,128)S(1)} %get-tuple-element.203, f32[16,65,192]{2,0,1:T(8,128)S(1)} %get-tuple-element.125, f32[16,65,192]{2,0,1:T(8,128)S(1)} %get-tuple-element.124, f32[16]{0:T(128)S(1)} %get-tuple-element.168, f32[16]{0:T(128)S(1)} %get-tuple-element.169, ...), kind=kLoop, calls=%fused_computation.248 | loop fusion | flops 7995392 | bytes 10749632 | tf_op jit(solution)/shard_map/add | solution.py:36
  76.7 1.8 fusion.98
  78.6 3.0 %multiply_reduce_fusion.18 = (f32[16]{0:T(128)S(1)}, f32[16]{0:T(128)S(1)}, f32[16]{0:T(128)S(1)}, f32[16]{0:T(128)S(1)}, f32[16]{0:T(128)S(1)}, /*index=5*/f32[...) fusion(f32[16,65,192]{2,0,1:T(8,128)S(1)} %get-tuple-element.12, ...), kind=kOutput, calls=%fused_computation.210 | convolution fusion | flops 29884128 | bytes 10487936 | tf_op jit(solution)/shard_map/oc,owt->cwt/dot_general | solution.py:108
  81.6 1.1 fusion.102
  82.8 2.5 %collective-permute-start.8 = (f32[16,64,32]{2,0,1:T(8,128)}, f32[16,64,32]{2,0,1:T(8,128)}, u32[]{:S(2)}, u32[]{:S(2)}) collective-permute-start(f32[16,64,32]{2,0,1:T(8,128)} %get-tuple-element.134), channel_id=1, source_target_pairs={{0,8},{8,16},{16,24},{24,32},{32,40},{40,48},{48,56},{56,64},{64,7... | collective-permute-start | bytes 393224 | tf_op jit(solution)/shard_map/ppermute | solution.py:18
  85.3 2.1 collective-permute-start.9
  87.5 5.1 %multiply_reduce_fusion.9 = (f32[16]{0:T(128)S(1)}, f32[16]{0:T(128)S(1)}, f32[16]{0:T(128)S(1)}, f32[16]{0:T(128)S(1)}, f32[16]{0:T(128)S(1)}, /*index=5*/f32[1...) fusion(f32[16,64,128]{2,0,1:T(8,128)} %copy-done.3, f32[16,64,32]{2,0,1:T(8,128)} %copy-done.8, ...), kind=kLoop, calls=%fused_computation.201 | loop fusion | flops 3932016 | bytes 1835584 | tf_op jit(solution)/shard_map/reduce_sum | solution.py:55
  92.6 2.0 convolution_bitcast_fusion.2
  94.6 2.4 %collective-permute-done.8 = f32[16,64,32]{2,0,1:T(8,128)} collective-permute-done((f32[16,64,32]{2,0,1:T(8,128)}, f32[16,64,32]{2,0,1:T(8,128)}, u32[]{:S(2)}, u32[]{:S(2)}) %collective-permute-start.8) | collective-permute-done | bytes 131104 | tf_op jit(solution)/shard_map/ppermute | solution.py:18
  97.1 3.8 %collective-permute-done.9 = f32[16,64,32]{2,0,1:T(8,128)} collective-permute-done((f32[16,64,32]{2,0,1:T(8,128)}, f32[16,64,32]{2,0,1:T(8,128)}, u32[]{:S(2)}, u32[]{:S(2)}) %collective-permute-start.9) | collective-permute-done | bytes 131104 | tf_op jit(solution)/shard_map/ppermute | solution.py:21
  101.7 1.9 collective-permute-start.10
  103.6 7.6 %collective-permute-start.11 = (f32[16,1,192]{2,0,1:T(8,128)S(1)}, f32[16,1,192]{2,0,1:T(8,128)S(1)}, u32[]{:S(2)}, u32[]{:S(2)}) collective-permute-start(f32[16,1,192]{2,0,1:T(8,128)S(1)} %get-tuple-element.123), channel_id=1, source_target_pairs={{1,0},{2,1},{3,2},{4,3},{5,4},{6,5},{7,6},{9,8},{10,9},{11,10},{12... | collective-permute-start | bytes 36872 | tf_op jit(solution)/shard_map/ppermute | solution.py:21
  111.6 2.0 copy.56
  113.6 2.5 %maximum_maximum_fusion.2 = (f32[16,65,192]{2,0,1:T(8,128)S(1)}, f32[16,65,192]{2,0,1:T(8,128)S(1)}) fusion(f32[16,64,32]{2,0,1:T(8,128)} %collective-permute-done.9, f32[16,64,128]{2,0,1:T(8,128)S(1)} %copy-done.4, f32[16,64,32]{2,0,1:T(8,128)} %collective-permute-done.8, f32[16,1,192]{2,0,1:T(8,128)S(1)} %collective-permute-done.10, ...), kind=kLoop, calls=%fused_computation.54 | loop fusion | flops 1198080 | bytes 2408448 | tf_op jit(solution)/shard_map/concatenate | solution.py:22
  116.1 6.5 %fusion.99 = (f32[16]{0:T(128)S(1)}, f32[16,64,128]{2,0,1:T(8,128)S(1)}) fusion(f32[16,64,128]{2,0,1:T(8,128)S(1)} %copy-done.15, f32[16,65,192]{2,0,1:T(8,128)S(1)} %get-tuple-element.121, f32[16]{0:T(128)S(1)} %get-tuple-element.143, f32[16]{0:T(128)S(1)} %get-tuple-element.162, f32[16]{0:T(128)S(1)} %get-tuple-element.167, f32[16]{0:T(128)S(1)} %get-tuple-element.166, ...), kind=kLoop, calls=%fused_computation.333 | loop fusion | flops 9175024 | bytes 11273984 | tf_op jit(solution)/shard_map/reduce_sum | solution.py:115
  123.4 3.0 %multiply_reduce_fusion.45 = (f32[16]{0:T(128)S(1)}, f32[16]{0:T(128)S(1)}, f32[16]{0:T(128)S(1)}, f32[16]{0:T(128)S(1)}, f32[16]{0:T(128)S(1)}, /*index=5*/f32[...) fusion(f32[16,65,192]{2,0,1:T(8,128)S(1)} %get-tuple-element.12, ...), kind=kOutput, calls=%fused_computation.237 | convolution fusion | flops 29884128 | bytes 10487936 | tf_op jit(solution)/shard_map/oc,owt->cwt/dot_general | solution.py:116
  126.5 1.1 fusion.101
  128.4 1.9 multiply_reduce_fusion.36
  130.7 1.8 all-gather.4
  132.5 9.1 %all-gather.5 = f32[4,1,1408]{2,1,0:T(1,128)S(1)} all-gather(f32[1,1,1408]{2,1,0:T(1,128)S(1)} %reshape.68), channel_id=3, replica_groups=mesh['y'=8,'z_hi'=4,'core'=2,'z_lo'=2,'x'=4] {'x'}, dimensions={0}, use_global_device_ids=true | all-gather | bytes 28160 | tf_op jit(solution)/shard_map/all_gather | solution.py:126
  141.6 21.4 %all-gather.6 = f32[8,1,1408]{2,1,0:T(1,128)S(1)} all-gather(f32[1,1,1408]{2,1,0:T(1,128)S(1)} %reshape.70), channel_id=4, replica_groups=mesh['y'=8,'z_hi'=4,'core'=2,'z_lo'=2,'x'=4] {'z_hi','z_lo'}, dimensions={0}, use_global_device_ids=true | all-gather | bytes 50688 | tf_op jit(solution)/shard_map/all_gather | solution.py:126
  163.1 18.3 %all-gather.7 = f32[8,1,1408]{2,1,0:T(1,128)S(1)} all-gather(f32[1,1,1408]{2,1,0:T(1,128)S(1)} %reshape.72), channel_id=5, replica_groups=mesh['y'=8,'z_hi'=4,'core'=2,'z_lo'=2,'x'=4] {'y'}, dimensions={0}, use_global_device_ids=true | all-gather | bytes 50688 | tf_op jit(solution)/shard_map/all_gather | solution.py:126
  181.5 17.5 %collective-permute-start.12 = (f32[16,64,32]{2,0,1:T(8,128)}, f32[16,64,32]{2,0,1:T(8,128)S(1)}, u32[]{:S(2)}, u32[]{:S(2)}) collective-permute-start(f32[16,64,32]{2,0,1:T(8,128)} %get-tuple-element.132), channel_id=1, source_target_pairs={{0,8},{8,16},{16,24},{24,32},{32,40},{40,48},{48,56},{56,64},{64,7... | collective-permute-start | bytes 393224 | tf_op jit(solution)/shard_map/ppermute | solution.py:18
  199.0 2.0 collective-permute-start.13
  201.1 9.4 %collective-permute-done.12 = f32[16,64,32]{2,0,1:T(8,128)S(1)} collective-permute-done((f32[16,64,32]{2,0,1:T(8,128)}, f32[16,64,32]{2,0,1:T(8,128)S(1)}, u32[]{:S(2)}, u32[]{:S(2)}) %collective-permute-start.12) | collective-permute-done | bytes 131104 | tf_op jit(solution)/shard_map/ppermute | solution.py:18
  210.5 5.8 %collective-permute-done.13 = f32[16,64,32]{2,0,1:T(8,128)S(1)} collective-permute-done((f32[16,64,32]{2,0,1:T(8,128)}, f32[16,64,32]{2,0,1:T(8,128)S(1)}, u32[]{:S(2)}, u32[]{:S(2)}) %collective-permute-start.13) | collective-permute-done | bytes 131104 | tf_op jit(solution)/shard_map/ppermute | solution.py:21
  216.3 1.9 collective-permute-start.14
  218.3 6.3 %collective-permute-start.15 = (f32[16,1,192]{2,0,1:T(8,128)S(1)}, f32[16,1,192]{2,0,1:T(8,128)S(1)}, u32[]{:S(2)}, u32[]{:S(2)}) collective-permute-start(f32[16,1,192]{2,0,1:T(8,128)S(1)} %get-tuple-element.119), channel_id=1, source_target_pairs={{1,0},{2,1},{3,2},{4,3},{5,4},{6,5},{7,6},{9,8},{10,9},{11,10},{12... | collective-permute-start | bytes 36872 | tf_op jit(solution)/shard_map/ppermute | solution.py:21
  228.2 2.1 maximum_maximum_fusion.3
  230.4 4.5 %fusion.14 = f32[16,64,128]{2,0,1:T(8,128)S(1)} fusion(f32[16,64,128]{2,0,1:T(8,128)S(1)} %get-tuple-element.205, f32[16,64,32]{2,0,1:T(8,128)S(1)} %copy-done.10, f32[16,64,32]{2,0,1:T(8,128)S(1)} %collective-permute-done.12, f32[16,65,192]{2,0,1:T(8,128)S(1)} %get-tuple-element.117, f32[16,65,192]{2,0,1:T(8,128)S(1)} %get-tuple-element.116, ...), kind=kLoop, calls=%fused_computation.70 | loop fusion | flops 7995392 | bytes 10749632 | tf_op jit(solution)/shard_map/add | solution.py:36
  234.9 1.0 copy.57
  (98 shorter events, 9.7 us)
Async XLA Ops:
  0.6 76.1 %copy-start = (f32[16,16]{1,0:T(8,128)S(1)}, f32[16,16]{1,0:T(8,128)}, u32[]{:S(2)}) copy-start(f32[16,16]{1,0:T(8,128)} %param.13) | copy-start | bytes 3076
  2.0 8.5 %copy-start.17 = (f32[16,3,9]{0,1,2:T(4,128)S(1)}, f32[16,3,9]{0,1,2:T(4,128)}, u32[]{:S(2)}) copy-start(f32[16,3,9]{0,1,2:T(4,128)} %param.9) | copy-start | bytes 5188
  2.2 17.2 %collective-permute-start = (f32[16,64,32]{2,0,1:T(8,128)S(1)}, f32[16,64,32]{2,0,1:T(8,128)S(1)}, u32[]{:S(2)}, u32[]{:S(2)}) collective-permute-start(f32[16,64,32]{2,0,1:T(8,128)S(1)} %get-tuple-element.141), channel_id=1, source_target_pairs={{0,8},{8,16},{16,24},{24,32},{32,40},{40,48},{48,56},{56,64},{64,7... | collective-permute-start | bytes 393224 | tf_op jit(solution)/shard_map/ppermute | solution.py:18
  8.6 13.5 %collective-permute-start.1 = (f32[16,64,32]{2,0,1:T(8,128)S(1)}, f32[16,64,32]{2,0,1:T(8,128)S(1)}, u32[]{:S(2)}, u32[]{:S(2)}) collective-permute-start(f32[16,64,32]{2,0,1:T(8,128)S(1)} %get-tuple-element.142), channel_id=1, source_target_pairs={{8,0},{16,8},{24,16},{32,24},{40,32},{48,40},{56,48},{64,56},{72,6... | collective-permute-start | bytes 393224 | tf_op jit(solution)/shard_map/ppermute | solution.py:21
  19.5 15.9 %copy-start.5 = (f32[16,64,32]{2,0,1:T(8,128)}, f32[16,64,32]{2,0,1:T(8,128)S(1)}, u32[]{:S(2)}) copy-start(f32[16,64,32]{2,0,1:T(8,128)S(1)} %collective-permute-done) | copy-start | bytes 393220
  22.2 11.6 %collective-permute-start.2 = (f32[16,1,192]{2,0,1:T(8,128)S(1)}, f32[16,1,192]{2,0,1:T(8,128)S(1)}, u32[]{:S(2)}, u32[]{:S(2)}) collective-permute-start(f32[16,1,192]{2,0,1:T(8,128)S(1)} %get-tuple-element.130), channel_id=1, source_target_pairs={{0,1},{1,2},{2,3},{3,4},{4,5},{5,6},{6,7},{8,9},{9,10},{10,11},{11... | collective-permute-start | bytes 36872 | tf_op jit(solution)/shard_map/ppermute | solution.py:18
  25.3 9.2 %collective-permute-start.3 = (f32[16,1,192]{2,0,1:T(8,128)S(1)}, f32[16,1,192]{2,0,1:T(8,128)S(1)}, u32[]{:S(2)}, u32[]{:S(2)}) collective-permute-start(f32[16,1,192]{2,0,1:T(8,128)S(1)} %get-tuple-element.131), channel_id=1, source_target_pairs={{1,0},{2,1},{3,2},{4,3},{5,4},{6,5},{7,6},{9,8},{10,9},{11,10},{12... | collective-permute-start | bytes 36872 | tf_op jit(solution)/shard_map/ppermute | solution.py:21
  33.7 1.7 copy-start.1
  35.4 4.0 %copy-start.20 = (f32[16,16]{1,0:T(8,128)S(1)}, f32[16,16]{1,0:T(8,128)}, u32[]{:S(2)}) copy-start(f32[16,16]{1,0:T(8,128)} %param.10) | copy-start | bytes 3076
  35.4 4.0 %copy-start.21 = (f32[16]{0:T(128)S(1)}, f32[16]{0:T(128)}, u32[]{:S(2)}) copy-start(f32[16]{0:T(128)} %param.11) | copy-start | bytes 196
  39.4 1.4 copy-start.12
  40.8 4.5 %copy-start.18 = (f32[16,3,9]{0,1,2:T(4,128)S(1)}, f32[16,3,9]{0,1,2:T(4,128)}, u32[]{:S(2)}) copy-start(f32[16,3,9]{0,1,2:T(4,128)} %param.12) | copy-start | bytes 5188
  41.0 13.7 %collective-permute-start.4 = (f32[16,64,32]{2,0,1:T(8,128)S(1)}, f32[16,64,32]{2,0,1:T(8,128)S(1)}, u32[]{:S(2)}, u32[]{:S(2)}) collective-permute-start(f32[16,64,32]{2,0,1:T(8,128)S(1)} %get-tuple-element.137), channel_id=1, source_target_pairs={{0,8},{8,16},{16,24},{24,32},{32,40},{40,48},{48,56},{56,64},{64,7... | collective-permute-start | bytes 393224 | tf_op jit(solution)/shard_map/ppermute | solution.py:18
  43.0 19.4 %collective-permute-start.5 = (f32[16,64,32]{2,0,1:T(8,128)S(1)}, f32[16,64,32]{2,0,1:T(8,128)S(1)}, u32[]{:S(2)}, u32[]{:S(2)}) collective-permute-start(f32[16,64,32]{2,0,1:T(8,128)S(1)} %get-tuple-element.138), channel_id=1, source_target_pairs={{8,0},{16,8},{24,16},{32,24},{40,32},{48,40},{56,48},{64,56},{72,6... | collective-permute-start | bytes 393224 | tf_op jit(solution)/shard_map/ppermute | solution.py:21
  54.7 17.4 %copy-start.7 = (f32[16,64,32]{2,0,1:T(8,128)}, f32[16,64,32]{2,0,1:T(8,128)S(1)}, u32[]{:S(2)}) copy-start(f32[16,64,32]{2,0,1:T(8,128)S(1)} %collective-permute-done.4) | copy-start | bytes 393220
  62.4 9.8 %copy-start.8 = (f32[16,64,32]{2,0,1:T(8,128)}, f32[16,64,32]{2,0,1:T(8,128)S(1)}, u32[]{:S(2)}) copy-start(f32[16,64,32]{2,0,1:T(8,128)S(1)} %collective-permute-done.5) | copy-start | bytes 393220
  62.5 8.0 %collective-permute-start.6 = (f32[16,1,192]{2,0,1:T(8,128)S(1)}, f32[16,1,192]{2,0,1:T(8,128)S(1)}, u32[]{:S(2)}, u32[]{:S(2)}) collective-permute-start(f32[16,1,192]{2,0,1:T(8,128)S(1)} %get-tuple-element.126), channel_id=1, source_target_pairs={{0,1},{1,2},{2,3},{3,4},{4,5},{5,6},{6,7},{8,9},{9,10},{10,11},{11... | collective-permute-start | bytes 36872 | tf_op jit(solution)/shard_map/ppermute | solution.py:18
  64.4 6.9 %collective-permute-start.7 = (f32[16,1,192]{2,0,1:T(8,128)S(1)}, f32[16,1,192]{2,0,1:T(8,128)S(1)}, u32[]{:S(2)}, u32[]{:S(2)}) collective-permute-start(f32[16,1,192]{2,0,1:T(8,128)S(1)} %get-tuple-element.127), channel_id=1, source_target_pairs={{1,0},{2,1},{3,2},{4,3},{5,4},{6,5},{7,6},{9,8},{10,9},{11,10},{12... | collective-permute-start | bytes 36872 | tf_op jit(solution)/shard_map/ppermute | solution.py:21
  72.2 4.5 %copy-start.19 = (f32[16,64,128]{2,1,0:T(8,128)S(1)}, f32[16,64,128]{2,1,0:T(8,128)}, u32[]{:S(2)}) copy-start(f32[16,64,128]{2,1,0:T(8,128)} %param.15) | copy-start | bytes 1572868
  72.2 4.5 %copy-start.22 = (f32[16]{0:T(128)S(1)}, f32[16]{0:T(128)}, u32[]{:S(2)}) copy-start(f32[16]{0:T(128)} %param.14) | copy-start | bytes 196
  76.7 1.8 copy-start.14
  78.5 3.0 %copy-start.16 = (f32[16,64,128]{2,0,1:T(8,128)}, f32[16,64,128]{2,0,1:T(8,128)S(1)}, u32[]{:S(2)}) copy-start(f32[16,64,128]{2,0,1:T(8,128)S(1)} %get-tuple-element.113) | copy-start | bytes 1572868
  81.6 5.8 %copy-start.3 = (f32[16,64,128]{2,0,1:T(8,128)}, f32[16,64,128]{2,0,1:T(8,128)S(1)}, u32[]{:S(2)}) copy-start(f32[16,64,128]{2,0,1:T(8,128)S(1)} %get-tuple-element.206) | copy-start | bytes 1572868
  82.8 14.3 %collective-permute-start.8 = (f32[16,64,32]{2,0,1:T(8,128)}, f32[16,64,32]{2,0,1:T(8,128)}, u32[]{:S(2)}, u32[]{:S(2)}) collective-permute-start(f32[16,64,32]{2,0,1:T(8,128)} %get-tuple-element.134), channel_id=1, source_target_pairs={{0,8},{8,16},{16,24},{24,32},{32,40},{40,48},{48,56},{56,64},{64,7... | collective-permute-start | bytes 393224 | tf_op jit(solution)/shard_map/ppermute | solution.py:18
  85.3 15.5 %collective-permute-start.9 = (f32[16,64,32]{2,0,1:T(8,128)}, f32[16,64,32]{2,0,1:T(8,128)}, u32[]{:S(2)}, u32[]{:S(2)}) collective-permute-start(f32[16,64,32]{2,0,1:T(8,128)} %get-tuple-element.135), channel_id=1, source_target_pairs={{8,0},{16,8},{24,16},{32,24},{40,32},{48,40},{56,48},{64,56},{72,6... | collective-permute-start | bytes 393224 | tf_op jit(solution)/shard_map/ppermute | solution.py:21
  92.5 8.3 %copy-start.4 = (f32[16,64,128]{2,0,1:T(8,128)S(1)}, f32[16,64,128]{2,0,1:T(8,128)}, u32[]{:S(2)}) copy-start(f32[16,64,128]{2,0,1:T(8,128)} %copy-done.3) | copy-start | bytes 1572868
  101.7 11.9 %collective-permute-start.10 = (f32[16,1,192]{2,0,1:T(8,128)S(1)}, f32[16,1,192]{2,0,1:T(8,128)S(1)}, u32[]{:S(2)}, u32[]{:S(2)}) collective-permute-start(f32[16,1,192]{2,0,1:T(8,128)S(1)} %get-tuple-element.122), channel_id=1, source_target_pairs={{0,1},{1,2},{2,3},{3,4},{4,5},{5,6},{6,7},{8,9},{9,10},{10,11},{11... | collective-permute-start | bytes 36872 | tf_op jit(solution)/shard_map/ppermute | solution.py:18
  103.6 10.0 %collective-permute-start.11 = (f32[16,1,192]{2,0,1:T(8,128)S(1)}, f32[16,1,192]{2,0,1:T(8,128)S(1)}, u32[]{:S(2)}, u32[]{:S(2)}) collective-permute-start(f32[16,1,192]{2,0,1:T(8,128)S(1)} %get-tuple-element.123), channel_id=1, source_target_pairs={{1,0},{2,1},{3,2},{4,3},{5,4},{6,5},{7,6},{9,8},{10,9},{11,10},{12... | collective-permute-start | bytes 36872 | tf_op jit(solution)/shard_map/ppermute | solution.py:21
  113.6 2.5 %copy-start.15 = (f32[16,64,128]{2,0,1:T(8,128)S(1)}, f32[16,64,128]{2,0,1:T(8,128)}, u32[]{:S(2)}) copy-start(f32[16,64,128]{2,0,1:T(8,128)} %get-tuple-element.204) | copy-start | bytes 1572868
  116.1 6.5 %copy-start.13 = (f32[16,64,128]{2,0,1:T(8,128)S(1)}, f32[16,64,128]{2,0,1:T(8,128)}, u32[]{:S(2)}) copy-start(f32[16,64,128]{2,0,1:T(8,128)} %copy-done.12) | copy-start | bytes 1572868
  126.5 1.6 copy-start.2
  126.5 1.7 copy-start.6
  126.5 1.9 copy-start.11
  181.5 29.0 %collective-permute-start.12 = (f32[16,64,32]{2,0,1:T(8,128)}, f32[16,64,32]{2,0,1:T(8,128)S(1)}, u32[]{:S(2)}, u32[]{:S(2)}) collective-permute-start(f32[16,64,32]{2,0,1:T(8,128)} %get-tuple-element.132), channel_id=1, source_target_pairs={{0,8},{8,16},{16,24},{24,32},{32,40},{40,48},{48,56},{56,64},{64,7... | collective-permute-start | bytes 393224 | tf_op jit(solution)/shard_map/ppermute | solution.py:18
  199.0 17.3 %collective-permute-start.13 = (f32[16,64,32]{2,0,1:T(8,128)}, f32[16,64,32]{2,0,1:T(8,128)S(1)}, u32[]{:S(2)}, u32[]{:S(2)}) collective-permute-start(f32[16,64,32]{2,0,1:T(8,128)} %get-tuple-element.133), channel_id=1, source_target_pairs={{8,0},{16,8},{24,16},{32,24},{40,32},{48,40},{56,48},{64,56},{72,6... | collective-permute-start | bytes 393224 | tf_op jit(solution)/shard_map/ppermute | solution.py:21
  216.3 11.9 %copy-start.9 = (f32[16,64,32]{2,0,1:T(8,128)}, f32[16,64,32]{2,0,1:T(8,128)S(1)}, u32[]{:S(2)}) copy-start(f32[16,64,32]{2,0,1:T(8,128)S(1)} %collective-permute-done.13) | copy-start | bytes 393220
  216.3 11.9 %collective-permute-start.14 = (f32[16,1,192]{2,0,1:T(8,128)S(1)}, f32[16,1,192]{2,0,1:T(8,128)S(1)}, u32[]{:S(2)}, u32[]{:S(2)}) collective-permute-start(f32[16,1,192]{2,0,1:T(8,128)S(1)} %get-tuple-element.118), channel_id=1, source_target_pairs={{0,1},{1,2},{2,3},{3,4},{4,5},{5,6},{6,7},{8,9},{9,10},{10,11},{11... | collective-permute-start | bytes 36872 | tf_op jit(solution)/shard_map/ppermute | solution.py:18
  218.3 9.9 %collective-permute-start.15 = (f32[16,1,192]{2,0,1:T(8,128)S(1)}, f32[16,1,192]{2,0,1:T(8,128)S(1)}, u32[]{:S(2)}, u32[]{:S(2)}) collective-permute-start(f32[16,1,192]{2,0,1:T(8,128)S(1)} %get-tuple-element.119), channel_id=1, source_target_pairs={{1,0},{2,1},{3,2},{4,3},{5,4},{6,5},{7,6},{9,8},{10,9},{11,10},{12... | collective-permute-start | bytes 36872 | tf_op jit(solution)/shard_map/ppermute | solution.py:21
  228.2 2.2 copy-start.10
